TPU v7x, 256 devices: a whole 4x4x8 slice. The times are simulated.
256 devices in a mesh: space: 128 (over y, z, x), dp: 2 (over core).
Axes of the slice: x: 4, y: 4, z: 8, core: 2. Of those that a mesh axis runs over, the one named last changes fastest.
Arguments:
- features: bfloat16 [1536, 8, 8, 512], P(('space', 'dp')), may hold values from -6 to 6
- grad_out: bfloat16 [1536, 8, 8, 512], P(('space', 'dp')), may hold values from -6 to 6
- occupancy: int32 [1536, 512], P(('space', 'dp')), may hold values 0 or 1
- weight: bfloat16 [3, 3, 3, 64, 64], replicated, may hold values from -0.15625 to 0.15625
- neighbours: int32 [1536, 26], P(('space', 'dp')), may hold values from 0 to 14, as said below
- send_rows: int32 [256, 4, 2], P(('space', 'dp')), may hold values from 0 to 6, as said below
Outputs:
- output: bfloat16 [1536, 8, 8, 512], P(('space', 'dp'))
- feature_grad: bfloat16 [1536, 8, 8, 512], P(('space', 'dp'))
- weight_grad: float32 [3, 3, 3, 64, 64], replicated
Inputs may be any that keep to these rules, and one draw needn't show every extreme that they name: `neighbours`: A value below 6 names another block of the same device; 6 + k * 2 + j names slot j of list k of the device k sends from, that is the device 1 lower, 1 higher, 2 lower, 2 higher along space for k = 0, 1, 2, 3 (same dp index); 14 names no block. Every filled slot of a list sent to a device is named by some entry of that device, and no unfilled slot is named. `send_rows`: list k of a device holds the blocks it sends to the device 1 higher, 1 lower, 2 higher, 2 lower along space for k = 0, 1, 2, 3 (same dp index); 6 marks an unfilled slot, filled slots come first and name distinct blocks; lists to devices outside the axis are unfilled.
All inputs are finite; a program needn't handle non-finite values. No bound on the sum of `occupancy` on one device may be relied on, other than what follows from the above.
Results may differ from a plain program's by a relative error of at most 0.003.
Values may be sent and summed in bfloat16 or wider, within the bound.
No kernel may reach another device: no remote copies, remote signals or barrier semaphores. Data moves between devices by JAX's collectives and lax.ppermute only.
A program may use at most 128 MiB of HBM per device.

v0:
```python
import functools
import math

import jax
import jax.numpy as jnp
from jax import lax
from jax.experimental import pallas as pl
from jax.experimental.pallas import tpu as pltpu
from jax.sharding import Mesh
from jax.sharding import PartitionSpec as P

STEPS = (1, 1, 2, 2)
FIRST = (0, 1, 0, 1)
OFFSETS = [
    (step_x, step_y, step_z)
    for step_x in (-1, 0, 1)
    for step_y in (-1, 0, 1)
    for step_z in (-1, 0, 1)
    if (step_x, step_y, step_z) != (0, 0, 0)
]
SLOT_OF = {offset: num for num, offset in enumerate(OFFSETS)}
BF16 = jnp.bfloat16
F32 = jnp.float32
NB = 6
CAP = 2
NT = NB + 4 * CAP + 1


SPACE = ("y", "z", "x")
PLANE = ("y", "x", "dp")


def swapped(block, step, first):
    count = lax.axis_size(SPACE)
    route = []
    for i in range(count):
        peer = i + step if (i // step) % 2 == first else i - step
        if 0 <= peer < count:
            route.append((i, peer))
    return lax.ppermute(block, SPACE, route)


def after(value, *others):
    return lax.optimization_barrier((value, *others))[0]


def dot(left, right, left_dim, right_dim):
    dims = (((left_dim,), (right_dim,)), ((), ()))
    return lax.dot_general(left, right, dims, preferred_element_type=F32)


def live_block(occ_row):
    voxel = lax.broadcasted_iota(jnp.int32, (64, 512), 1)
    line = lax.broadcasted_iota(jnp.int32, (64, 512), 0)
    left = jnp.where(voxel // 8 == line, jnp.broadcast_to(occ_row, (64, 512)), 0)
    voxel = lax.broadcasted_iota(jnp.int32, (512, 512), 0)
    lane = lax.broadcasted_iota(jnp.int32, (512, 512), 1)
    spread = jnp.where(voxel % 8 == lane // 64, 1.0, 0.0)
    return dot(left.astype(F32).astype(BF16), spread.astype(BF16), 1, 0)


def lanes(t):
    return slice(128 * t, 128 * t + 128)


def outgoing(column):
    low = column[0] & 1
    high = column[0] >> 1
    return (low, 1 - low, 2 + high, 3 - high)


def incoming(column):
    low, other, high, last = outgoing(column)
    return (1 - low, 1 - other, 5 - high, 5 - last)


def prep_kernel(
    feat_far, grad_far, occ_far, send, column, shown, live, g, s0, s1, s2, s3,
    mask, feat, grad, occ, sems,
):
    copies = [pltpu.make_async_copy(occ_far, occ, sems.at[0])]
    for pair in range(NB // 2):
        part = pl.ds(2 * pair, 2)
        copies.append(
            pltpu.make_async_copy(feat_far.at[part], feat.at[part], sems.at[1 + pair])
        )
    copies.append(pltpu.make_async_copy(grad_far, grad, sems.at[1 + NB // 2]))
    for copy in copies:
        copy.start()
    copies[0].wait()
    for b in range(NB):
        mask[64 * b : 64 * b + 64, :] = live_block(occ[b : b + 1, :])
    for b in range(NB):
        if b % 2 == 0:
            copies[1 + b // 2].wait()
        for x in range(8):
            on = mask[b * 64 + x * 8 : b * 64 + x * 8 + 8, :]
            live[b, x] = on.astype(BF16)
            shown[b, x] = jnp.where(on > 0.5, feat[b, x].astype(F32), 0.0).astype(BF16)
    lists = outgoing(column)
    for n, out in enumerate((s0, s1, s2, s3)):
        for j in range(CAP):
            row = jnp.minimum(send[0, j, lists[n]], NB - 1)
            out[j] = shown[row]
    copies[-1].wait()
    for x in range(8):
        for pair in range(NB // 2):
            parts = []
            for b in (2 * pair, 2 * pair + 1):
                on = mask[b * 64 + x * 8 : b * 64 + x * 8 + 8, :] > 0.5
                parts.append(jnp.where(on, grad[b, x].astype(F32), 0.0))
            g[x, 16 * pair : 16 * pair + 16, :] = jnp.concatenate(parts, axis=0).astype(BF16)


def dgrad_kernel(g, wp, nbr, column, rloc, r0, r1, r2, r3, gext, wbt, dsc, acc):
    gext[0:96, :] = jnp.zeros((96, 768), BF16)
    gext[480:576, :] = jnp.zeros((96, 768), BF16)
    gext[96:480, 0:128] = jnp.zeros((384, 128), BF16)
    gext[96:480, 640:768] = jnp.zeros((384, 128), BF16)
    for x in range(8):
        gext[96 + 48 * x : 144 + 48 * x, 128:640] = g[x]
    for a in range(3):
        for c in range(3):
            for o in range(2):
                for s in range(2):
                    row = c * 128 + (1 - o) * 64
                    wbt[row : row + 64, a * 256 + s * 128 : a * 256 + s * 128 + 128] = wp[
                        (a * 3 + c) * 4 + o + 2 - 2 * s
                    ]
    for q in range(5):
        left = jnp.concatenate(
            [
                gext[(2 - a) * 48 : (2 - a) * 48 + 480, 128 * q : 128 * q + 256]
                for a in range(3)
            ],
            axis=1,
        )
        dsc[q] = dot(left, wbt[...], 1, 1)
    acc[...] = jnp.zeros((NT * 8, 8, 512), F32)
    low = lax.broadcasted_iota(jnp.int32, (8, 128), 1) < 64
    sub = lax.broadcasted_iota(jnp.int32, (8, 128), 0)

    def add_rows(b, offset, xs, tiles):
        def target(oz):
            if (offset[0], offset[1], oz) == (0, 0, 0):
                return b * 8 + xs
            return nbr[b, SLOT_OF[offset[0], offset[1], oz]] * 8 + xs

        row = target(0)
        for t in range(4):
            acc[row, :, lanes(t)] += tiles[t]
        row = target(1)
        acc[row, :, lanes(0)] += jnp.where(low, tiles[4], 0.0)
        row = target(-1)
        acc[row, :, lanes(3)] += jnp.where(low, 0.0, tiles[4])

    def group(xx, ox, xs):
        for b in range(NB):
            base = pl.multiple_of(xx * 48 + b * 8, 8)
            z = []
            for c in range(3):
                d = [dsc[t, pl.ds(base, 8), lanes(c)] for t in range(5)]
                z.append([jnp.where(low, d[t], d[(t + 1) % 5]) for t in range(5)])
            up = [pltpu.roll(v, 7, 0) for v in z[0]]
            down = [pltpu.roll(v, 1, 0) for v in z[2]]
            inner = [
                z[1][t] + jnp.where(sub < 7, up[t], 0.0) + jnp.where(sub > 0, down[t], 0.0)
                for t in range(5)
            ]
            add_rows(b, (ox, 0), xs, inner)
            add_rows(b, (ox, -1), xs, [jnp.where(sub == 7, v, 0.0) for v in up])
            add_rows(b, (ox, 1), xs, [jnp.where(sub == 0, v, 0.0) for v in down])

    group(0, -1, 7)

    def middle(x, carry):
        group(x + 1, 0, x)
        return carry

    lax.fori_loop(0, 8, middle, 0)
    group(9, 1, 0)
    rloc[...] = acc[0 : NB * 8]
    lists = incoming(column)
    for n, out in enumerate((r0, r1, r2, r3)):
        start = NB + CAP * lists[n]
        for j in range(CAP):
            for x in range(8):
                out[j, x] = acc[(start + j) * 8 + x].astype(BF16)


def widen_kernel(g, gext):
    sub = lax.broadcasted_iota(jnp.int32, (8, 128), 0)
    zero = jnp.zeros((8, 128), F32)
    gext[0:128, :] = jnp.zeros((128, 1536), BF16)
    gext[640:768, :] = jnp.zeros((128, 1536), BF16)

    def fill_g(x, carry):
        for p in range(4):
            cols = [p * 384 + c * 128 for c in range(3)]
            h_low, h_high = zero, zero
            base = pl.multiple_of((x + 2) * 64, 64)
            for pair in range(NB // 2):
                both = g[x, 16 * pair : 16 * pair + 16, lanes(p)]
                both32 = both.astype(F32)
                ups, downs = [], []
                for half in range(2):
                    b = 2 * pair + half
                    v = both32[8 * half : 8 * half + 8]
                    ups.append(jnp.where(sub < 7, pltpu.roll(v, 7, 0), 0.0))
                    downs.append(jnp.where(sub > 0, pltpu.roll(v, 1, 0), 0.0))
                    h_low = jnp.where(sub == b, pltpu.roll(v, b, 0) if b else v, h_low)
                    h_high = jnp.where(sub == b, pltpu.roll(v, b + 1, 0), h_high)
                rows = pl.ds(pl.multiple_of(base + 16 * pair, 16), 16)
                gext[rows, cols[0] : cols[0] + 128] = jnp.concatenate(ups, 0).astype(BF16)
                gext[rows, cols[1] : cols[1] + 128] = both
                gext[rows, cols[2] : cols[2] + 128] = jnp.concatenate(downs, 0).astype(BF16)
            rows = pl.ds(pl.multiple_of(base + 48, 16), 16)
            gext[rows, cols[0] : cols[0] + 128] = jnp.concatenate([h_low, zero], 0).astype(BF16)
            gext[rows, cols[1] : cols[1] + 128] = jnp.zeros((16, 128), BF16)
            gext[rows, cols[2] : cols[2] + 128] = jnp.concatenate([zero, h_high], 0).astype(BF16)
        return carry

    lax.fori_loop(0, 8, fill_g, 0)


def wgrad_kernel(shown, a0, a1, a2, a3, before, gext, nbr, column, px, dwp, table, dsc, sems):
    copies = [pltpu.make_async_copy(shown, table.at[0:NB], sems.at[0])]
    lists = incoming(column)
    for n, src in enumerate((a0, a1, a2, a3)):
        start = NB + CAP * lists[n]
        copies.append(pltpu.make_async_copy(src, table.at[pl.ds(start, CAP)], sems.at[n + 1]))
    for copy in copies:
        copy.start()
    low = lax.broadcasted_iota(jnp.int32, (8, 128), 1) < 64
    sub = lax.broadcasted_iota(jnp.int32, (8, 128), 0)
    zero = jnp.zeros((8, 128), F32)
    table[NT - 1] = jnp.zeros((8, 8, 512), BF16)
    for copy in copies:
        copy.wait()

    def windows(tiles):
        merged = [
            jnp.where(low, tiles[p + 1], tiles[(p + 4) % 5]) for p in range(4)
        ]
        return [v for p in range(4) for v in (tiles[p], merged[p])]

    def five(b, ox, oy, xs):
        def source(oz):
            if (ox, oy, oz) == (0, 0, 0):
                return table[b, xs].astype(F32)
            return table[nbr[b, SLOT_OF[ox, oy, oz]], xs].astype(F32)

        centre, after, before = source(0), source(1), source(-1)
        tiles = [centre[:, lanes(t)] for t in range(4)]
        return tiles + [jnp.where(low, after[:, lanes(0)], before[:, lanes(3)])]

    def fill_plane(xx, ox, xs):
        base = pl.multiple_of(xx * 64, 64)
        h_low, h_high = [zero] * 5, [zero] * 5
        for pair in range(NB // 2):
            wins = []
            for b in (2 * pair, 2 * pair + 1):
                wins.append(windows(five(b, ox, 0, xs)))
                v = five(b, ox, -1, xs)
                h_low = [
                    jnp.where(sub == b, pltpu.roll(v[t], b + 1, 0), h_low[t]) for t in range(5)
                ]
                v = five(b, ox, 1, xs)
                h_high = [
                    jnp.where(sub == b, pltpu.roll(v[t], b, 0) if b else v[t], h_high[t])
                    for t in range(5)
                ]
            rows = pl.ds(pl.multiple_of(base + 16 * pair, 16), 16)
            for n in range(8):
                px[rows, lanes(n)] = jnp.concatenate([wins[0][n], wins[1][n]], 0).astype(BF16)
        wins = [windows(h_low), windows(h_high)]
        rows = pl.ds(pl.multiple_of(base + 48, 16), 16)
        for n in range(8):
            px[rows, lanes(n)] = jnp.concatenate([wins[0][n], wins[1][n]], 0).astype(BF16)

    fill_plane(0, -1, 7)

    def middle_fill(x, carry):
        fill_plane(x + 1, 0, x)
        return carry

    lax.fori_loop(0, 8, middle_fill, 0)
    fill_plane(9, 1, 0)

    for p in range(4):
        right = jnp.concatenate(
            [
                gext[(2 - a) * 64 : (2 - a) * 64 + 640, p * 384 : p * 384 + 384]
                for a in range(3)
            ],
            axis=1,
        )
        part = dot(px[:, 256 * p : 256 * p + 256], right, 0, 0)
        if p == 0:
            dsc[...] = part
        else:
            dsc[...] += part
    low64 = lax.broadcasted_iota(jnp.int32, (64, 128), 1) < 64
    row_of = (192, 0, 64, 128)
    taps = [(a, c, e) for a in range(3) for c in range(3) for e in range(3)]

    def tap_parts(tap):
        a, c, e = tap
        col = a * 384 + c * 128
        first = dsc[row_of[e] : row_of[e] + 64, col : col + 128]
        second = dsc[row_of[e + 1] : row_of[e + 1] + 64, col : col + 128]
        return first, second

    for n in range(14):
        first, second = tap_parts(taps[2 * n])
        left = first + pltpu.roll(second, 64, 1)
        if 2 * n + 1 < 27:
            first, second = tap_parts(taps[2 * n + 1])
            right = second + pltpu.roll(first, 64, 1)
        else:
            right = jnp.zeros((64, 128), F32)
        dwp[64 * n : 64 * n + 64, :] = jnp.where(low64, left, right)
    dwp[896:1024, :] = jnp.zeros((128, 128), F32)


def conv_kernel(px, wp, live, out, wf, gsc):
    sub = lax.broadcasted_iota(jnp.int32, (8, 128), 0)
    for a in range(3):
        for c in range(3):
            for n, t in enumerate((1, 2, 3, 0)):
                row = a * 256 + n * 64
                wf[row : row + 64, lanes(c)] = wp[(a * 3 + c) * 4 + t]
    for p in range(4):
        left = jnp.concatenate(
            [px[64 * a : 64 * a + 512, 256 * p : 256 * p + 256] for a in range(3)], axis=1
        )
        gsc[p] = dot(left, wf[...], 1, 0)

    def finish(x, carry):
        base = pl.multiple_of(x * 64, 64)
        for p in range(4):
            lo_rows = gsc[p, pl.ds(pl.multiple_of(base + 48, 8), 8), lanes(0)]
            hi_rows = gsc[p, pl.ds(pl.multiple_of(base + 56, 8), 8), lanes(2)]
            for b in range(NB):
                rows = pl.ds(pl.multiple_of(base + 8 * b, 8), 8)
                v = [gsc[p, rows, lanes(c)] for c in range(3)]
                lo = pltpu.roll(lo_rows, (8 - b) % 8, 0) if b else lo_rows
                hi = pltpu.roll(hi_rows, 7 - b, 0)
                total = (
                    v[1]
                    + jnp.where(sub > 0, pltpu.roll(v[0], 1, 0), lo)
                    + jnp.where(sub < 7, pltpu.roll(v[2], 7, 0), hi)
                )
                on = live[b, x, :, lanes(p)].astype(F32)
                out[b, x, :, lanes(p)] = (total * on).astype(BF16)
        return carry

    lax.fori_loop(0, 8, finish, 0)


def final_kernel(rloc, a0, a1, a2, a3, live, send, column, out, acc):
    acc[...] = rloc[...]
    lists = outgoing(column)
    for n, src in enumerate((a0, a1, a2, a3)):
        for j in range(CAP):
            row = send[0, j, lists[n]]

            @pl.when(row < NB)
            def _(src=src, j=j, row=row):
                for x in range(8):
                    acc[row * 8 + x] += src[j, x].astype(F32)

    for x in range(8):
        for b in range(NB):
            out[b, x] = (acc[b * 8 + x] * live[b, x].astype(F32)).astype(BF16)


def sum_kernel(parts, out, *, scale):
    total = parts[0]
    for n in range(1, parts.shape[0]):
        total = total + parts[n]
    total = total * scale
    for n in range(out.shape[0]):
        out[n] = total


def unpack_kernel(packed, out):
    for n in range(14):
        tile = packed[64 * n : 64 * n + 64, :]
        out[2 * n] = tile[:, 0:64]
        if 2 * n + 1 < 27:
            out[2 * n + 1] = pltpu.roll(tile, 64, 1)[:, 0:64]


def in_vmem(x):
    return pltpu.with_memory_space_constraint(x, pltpu.VMEM)


def in_hbm(x):
    return pltpu.with_memory_space_constraint(x, pltpu.HBM)


VM = pl.BlockSpec(memory_space=pltpu.VMEM)
SM = pl.BlockSpec(memory_space=pltpu.SMEM)
HBM = pl.BlockSpec(memory_space=pltpu.HBM)
BLOCK = jax.ShapeDtypeStruct((NB, 8, 8, 512), BF16)
HELD = pltpu.VMEM((NB, 8, 8, 512), BF16)
SEND = pltpu.VMEM((CAP, 8, 8, 512), BF16)


def call(kernel, ins, outs, scratch=(), **params):
    return pl.pallas_call(
        kernel,
        out_shape=outs,
        in_specs=ins,
        out_specs=[VM] * len(outs) if isinstance(outs, tuple) else VM,
        scratch_shapes=list(scratch),
        compiler_params=pltpu.CompilerParams(vmem_limit_bytes=20 << 20),
        **params,
    )


def reduced(parts, copies, scale):
    rows = parts.shape[1]
    out = pltpu.VMEM((copies, rows, 128), F32)
    kernel = functools.partial(sum_kernel, scale=scale)
    return call(kernel, [VM], out)(in_vmem(parts))


def weight_pass(shown, arrived, rloc, gext, neighbours, column):
    shape = jax.ShapeDtypeStruct
    return call(
        wgrad_kernel,
        [VM] * 7 + [SM, SM],
        (shape((640, 1024), BF16), pltpu.VMEM((1024, 128), F32)),
        [
            pltpu.VMEM((NT, 8, 8, 512), BF16),
            pltpu.VMEM((256, 1152), F32),
            pltpu.SemaphoreType.DMA((5,)),
        ],
    )(in_vmem(shown), *map(in_vmem, arrived), in_vmem(rloc), in_vmem(gext), neighbours, column)


def on_device(features, grad_out, occupancy, weight, neighbours, send_rows):
    shape = jax.ShapeDtypeStruct
    column = lax.axis_index("x").reshape(1)
    send_rows = jnp.transpose(send_rows, (0, 2, 1))
    shown, live, g, *sends = call(
        prep_kernel,
        [HBM, HBM, HBM, SM, SM],
        (HELD, HELD, pltpu.VMEM((8, 48, 512), BF16), SEND, SEND, SEND, SEND),
        [
            pltpu.VMEM((NB * 64, 512), F32),
            pltpu.VMEM((NB, 8, 8, 512), BF16),
            pltpu.VMEM((NB, 8, 8, 512), BF16),
            pltpu.VMEM((NB, 512), jnp.int32),
            pltpu.SemaphoreType.DMA((NB // 2 + 2,)),
        ],
    )(in_hbm(features), in_hbm(grad_out), in_hbm(occupancy), send_rows, column)

    def swap(n, block):
        return swapped(block, STEPS[n], FIRST[n])

    arrived = [swap(0, sends[0])]
    arrived.append(swap(1, sends[1]))
    w = weight.reshape(9, 3, 64, 64)
    none = jnp.zeros((9, 1, 64, 64), BF16)
    wp = jnp.concatenate(
        [jnp.concatenate([w, none], axis=1), jnp.concatenate([none, w], axis=1)], axis=3
    ).reshape(36, 64, 128)
    arrived.append(swap(2, after(sends[2], wp)))
    rloc, *backs = call(
        dgrad_kernel,
        [VM, VM, SM, SM],
        (pltpu.VMEM((NB * 8, 8, 512), F32), SEND, SEND, SEND, SEND),
        [
            pltpu.VMEM((576, 768), BF16),
            pltpu.VMEM((384, 768), BF16),
            pltpu.VMEM((5, 480, 384), F32),
            pltpu.VMEM((NT * 8, 8, 512), F32),
        ],
    )(in_vmem(g), in_vmem(wp), neighbours, column)
    arrived.append(swap(3, after(sends[3], rloc)))
    gext = call(widen_kernel, [VM], pltpu.VMEM((768, 1536), BF16))(in_vmem(after(g, rloc)))
    returned = {}
    for n in (0, 2):
        returned[n] = swap(n, after(backs[n], gext))
    px, dwp = weight_pass(shown, arrived, rloc, gext, neighbours, column)

    count = lax.axis_size(SPACE) * lax.axis_size("dp")
    scale = 1.0 / math.sqrt(count * NB * 512)
    near = lax.axis_size(PLANE)
    far = count // near
    rows = 1024 // near
    parts = lax.all_to_all(dwp.reshape(near, rows, 128), PLANE, 0, 0, tiled=True)
    returned[1] = swap(1, after(backs[1], dwp))
    total = reduced(parts, far, 1.0)
    parts = lax.all_to_all(total, "z", 0, 0, tiled=True)
    returned[3] = swap(3, after(backs[3], total))
    total = reduced(parts, near, scale)
    packed = lax.all_to_all(total, PLANE, 0, 0, tiled=True).reshape(1024, 128)
    output = call(
        conv_kernel, [VM] * 3, BLOCK, [pltpu.VMEM((768, 384), BF16), pltpu.VMEM((4, 512, 384), F32)]
    )(in_hbm(px), in_vmem(wp), in_vmem(live))
    weight_grad = call(unpack_kernel, [VM], shape((27, 64, 64), F32))(in_vmem(packed))
    feature_grad = call(
        final_kernel, [VM] * 6 + [SM, SM], BLOCK, [pltpu.VMEM((NB * 8, 8, 512), F32)]
    )(in_vmem(rloc), *(in_vmem(returned[n]) for n in range(4)), in_vmem(live), send_rows, column)
    return (output, feature_grad, weight_grad.reshape(3, 3, 3, 64, 64))


def solution(mesh):
    grid = Mesh(mesh.devices.reshape(4, -1, 4, 2), ("y", "z", "x", "dp"))
    every = ("y", "z", "x", "dp")

    return jax.shard_map(
        on_device,
        mesh=grid,
        in_specs=(
            P(every, None, None, None),
            P(every, None, None, None),
            P(every, None),
            P(),
            P(every, None),
            P(every, None, None),
        ),
        out_specs=(P(every, None, None, None), P(every, None, None, None), P()),
        check_vma=False,
    )
```

profile of v0, /device:TPU:1, one launch (start us, length us, event | category | flops | bytes accessed | tf_op | source)
XLA Modules:
  0.0 96.2 jit_solution(11193048081780486952)
XLA Ops:
  0.6 0.0 copy-start.1
  0.6 1.6 %fusion.2 = bf16[9,4,64,128]{3,2,1,0:T(8,128)(2,1)S(1)} fusion(bf16[9,3,64,64]{3,2,1,0:T(8,128)(2,1)} %bitcast.14), kind=kLoop, calls=%fused_computation.4 | loop fusion | flops 2359296 | bytes 811008 | tf_op jit(solution)/shard_map/concatenate | solution.py:468
  2.2 0.0 copy-start.2
  2.3 0.7 copy-done.2
  2.9 2.2 %shard_map.85 = (bf16[6,8,8,512]{3,2,1,0:T(8,128)(2,1)S(1)}, bf16[6,8,8,512]{3,2,1,0:T(8,128)(2,1)S(1)}, bf16[8,48,512]{2,1,0:T(8,128)(2,1)S(1)}, bf16[2,8,8,512...) custom-call(bf16[6,8,8,512]{3,2,1,0:T(8,128)(2,1)} %feat_far.1, ...), custom_call_target="tpu_custom_call" | custom-call | tf_op jit(solution)/shard_map/pallas_call | solution.py:448
  5.2 3.6 %collective-permute-start.2 = (bf16[2,8,8,512]{3,2,1,0:T(8,128)(2,1)S(1)}, bf16[2,8,8,512]{3,2,1,0:T(8,128)(2,1)S(1)}, u32[]{:S(2)}, u32[]{:S(2)}) collective-permute-start(bf16[2,8,8,512]{3,2,1,0:T(8,128)(2,1)S(1)} %get-tuple-element.28), channel_id=1, source_target_pairs={{0,4},{2,6},{4,0},{6,2},{8,12},{10,14},{12,8},{14,10},{16,20},{18,... | collective-permute-start | bytes 393224 | tf_op jit(solution)/shard_map/ppermute | solution.py:40
  8.8 0.3 collective-permute-start
  9.1 0.7 collective-permute-start.1
  9.8 0.0 copy-done.1
  9.8 5.1 %shard_map.86 = (f32[48,8,512]{2,1,0:T(8,128)S(1)}, bf16[2,8,8,512]{3,2,1,0:T(8,128)(2,1)S(1)}, bf16[2,8,8,512]{3,2,1,0:T(8,128)(2,1)S(1)}, bf16[2,8,8,512]{3,2,1,0:T(8,128)(2,1)S(1)}, bf16[2,8,8,512]{3,2,1,0:T(8,128)(2,1)S(1)}) custom-call(bf16[8,48,512]{2,1,0:T(8,128)(2,1)S(1)} %get-tuple-element.33.g, bf16[36,64,128]{2,1,0:T(8,128)(2,1)S(1)} %bitcast.7, ...), custom_call_target="tpu_custom_call" | custom-call | tf_op jit(solution)/shard_map/pallas_call | solution.py:472
  14.9 0.7 collective-permute-start.3
  15.6 0.5 shard_map.87.gext
  16.0 0.0 collective-permute-done.2.a2
  16.1 0.0 collective-permute-done.a0
  16.1 0.0 collective-permute-done.1.a1
  16.1 0.0 collective-permute-done.3.a3
  16.1 4.4 %shard_map.88 = (bf16[640,1024]{1,0:T(8,128)(2,1)S(1)}, f32[1024,128]{1,0:T(8,128)S(1)}) custom-call(bf16[6,8,8,512]{3,2,1,0:T(8,128)(2,1)S(1)} %get-tuple-element.24.shown, bf16[2,8,8,512]{3,2,1,0:T(8,128)(2,1)S(1)} %collective-permute-done.a0, bf16[2,8,8,512]{3,2,1,0:T(8,128)(2,1)S(1)} %collective-permute-done.1.a1, ...), custom_call_target="tpu_custom_call" | custom-call | tf_op jit(solution)/shard_map/pallas_call | solution.py:432
  20.5 0.0 copy-start
  20.5 34.4 %all_to_all.15.parts = f32[32,32,128]{2,1,0:T(8,128)S(1)} all-to-all(f32[32,32,128]{2,1,0:T(8,128)S(1)} %bitcast.10), channel_id=1, replica_groups=mesh['y'=4,'z'=8,'x'=4,'dp'=2] {'y','x','dp'}, dimensions={0} | all-to-all | bytes 1048576 | tf_op jit(solution)/shard_map/all_to_all | solution.py:495
  54.9 0.0 copy-done
  55.0 11.8 %all_to_all.16.parts = f32[8,32,128]{2,1,0:T(8,128)S(1)} all-to-all(f32[8,32,128]{2,1,0:T(8,128)S(1)} %shard_map.90), channel_id=1, replica_groups=mesh['y'=4,'z'=8,'x'=4,'dp'=2] {'z'}, dimensions={0} | all-to-all | bytes 262144 | tf_op jit(solution)/shard_map/all_to_all | solution.py:498
  66.7 0.9 shard_map.92
  67.6 5.9 %all-to-all-start.2 = ((f32[32,32,128]{2,1,0:T(8,128)}), f32[32,32,128]{2,1,0:T(8,128)S(1)}, u32[]{:S(2)}, u32[]{:S(2)}) async-start(f32[32,32,128]{2,1,0:T(8,128)} %shard_map.92), calls=%async_computation.2 | async-start | bytes 1048576 | tf_op jit(solution)/shard_map/all_to_all | solution.py:501
  73.5 1.4 %collective-permute-start.4 = (bf16[2,8,8,512]{3,2,1,0:T(8,128)(2,1)S(1)}, bf16[2,8,8,512]{3,2,1,0:T(8,128)(2,1)S(1)}, u32[]{:S(2)}, u32[]{:S(2)}) collective-permute-start(bf16[2,8,8,512]{3,2,1,0:T(8,128)(2,1)S(1)} %get-tuple-element.37), channel_id=1, source_target_pairs={{0,2},{2,0},{4,6},{6,4},{8,10},{10,8},{12,14},{14,12},{16,18},{18,... | collective-permute-start | bytes 393224 | tf_op jit(solution)/shard_map/ppermute | solution.py:40
  74.9 2.4 %collective-permute-start.6 = (bf16[2,8,8,512]{3,2,1,0:T(8,128)(2,1)S(1)}, bf16[2,8,8,512]{3,2,1,0:T(8,128)(2,1)S(1)}, u32[]{:S(2)}, u32[]{:S(2)}) collective-permute-start(bf16[2,8,8,512]{3,2,1,0:T(8,128)(2,1)S(1)} %get-tuple-element.42), channel_id=1, source_target_pairs={{0,4},{2,6},{4,0},{6,2},{8,12},{10,14},{12,8},{14,10},{16,20},{18,... | collective-permute-start | bytes 393224 | tf_op jit(solution)/shard_map/ppermute | solution.py:40
  77.3 0.7 collective-permute-start.5
  78.0 0.7 collective-permute-start.7
  78.6 0.0 copy-start.3
  78.6 4.3 %shard_map.89 = bf16[6,8,8,512]{3,2,1,0:T(8,128)(2,1)} custom-call(bf16[640,1024]{1,0:T(8,128)(2,1)} %copy-done, bf16[36,64,128]{2,1,0:T(8,128)(2,1)S(1)} %bitcast.8, bf16[6,8,8,512]{3,2,1,0:T(8,128)(2,1)S(1)} %get-tuple-element.35.live), custom_call_target="tpu_custom_call" | custom-call | tf_op jit(solution)/shard_map/pallas_call | solution.py:502
  82.9 1.1 %collective-permute-done.4.a0 = bf16[2,8,8,512]{3,2,1,0:T(8,128)(2,1)S(1)} collective-permute-done((bf16[2,8,8,512]{3,2,1,0:T(8,128)(2,1)S(1)}, bf16[2,8,8,512]{3,2,1,0:T(8,128)(2,1)S(1)}, u32[]{:S(2)}, u32[]{:S(2)}) %collective-permute-start.4) | collective-permute-done | bytes 131104 | tf_op jit(solution)/shard_map/ppermute | solution.py:40
  84.0 9.6 %collective-permute-done.6.a2 = bf16[2,8,8,512]{3,2,1,0:T(8,128)(2,1)S(1)} collective-permute-done((bf16[2,8,8,512]{3,2,1,0:T(8,128)(2,1)S(1)}, bf16[2,8,8,512]{3,2,1,0:T(8,128)(2,1)S(1)}, u32[]{:S(2)}, u32[]{:S(2)}) %collective-permute-start.6) | collective-permute-done | bytes 131104 | tf_op jit(solution)/shard_map/ppermute | solution.py:40
  93.6 0.0 collective-permute-done.5.a1
  93.6 0.0 collective-permute-done.7.a3
  93.6 0.0 copy-done.3
  93.6 1.5 %shard_map.91 = bf16[6,8,8,512]{3,2,1,0:T(8,128)(2,1)} custom-call(f32[48,8,512]{2,1,0:T(8,128)S(1)} %get-tuple-element.31.before.rloc, bf16[2,8,8,512]{3,2,1,0:T(8,128)(2,1)S(1)} %collective-permute-done.4.a0, bf16[2,8,8,512]{3,2,1,0:T(8,128)(2,1)S(1)} %collective-permute-done.5.a1, bf16[2,8,8,512]{3,2,1,0:T(8,128)(2,1)S(1)} %collective-permute-done.6.a2, ...), custom_call_target="tpu_custom_call" | custom-call | tf_op jit(solution)/shard_map/pallas_call | solution.py:506
  95.1 0.0 all-to-all-done.2
  95.1 1.1 %shard_map.93 = f32[27,64,64]{2,1,0:T(8,128)} custom-call(f32[1024,128]{1,0:T(8,128)S(1)} %bitcast.9), custom_call_target="tpu_custom_call" | custom-call | tf_op jit(solution)/shard_map/pallas_call | solution.py:505
  (1 shorter events, 0.0 us)
Async XLA Ops:
  0.6 9.2 %copy-start.1 = (s32[6,26]{1,0:T(8,128)S(1)}, s32[6,26]{1,0:T(8,128)}, u32[]{:S(2)}) copy-start(s32[6,26]{1,0:T(8,128)} %nbr.3) | copy-start | bytes 1876
  2.2 0.7 copy-start.2
  5.2 10.9 %collective-permute-start.2 = (bf16[2,8,8,512]{3,2,1,0:T(8,128)(2,1)S(1)}, bf16[2,8,8,512]{3,2,1,0:T(8,128)(2,1)S(1)}, u32[]{:S(2)}, u32[]{:S(2)}) collective-permute-start(bf16[2,8,8,512]{3,2,1,0:T(8,128)(2,1)S(1)} %get-tuple-element.28), channel_id=1, source_target_pairs={{0,4},{2,6},{4,0},{6,2},{8,12},{10,14},{12,8},{14,10},{16,20},{18,... | collective-permute-start | bytes 393224 | tf_op jit(solution)/shard_map/ppermute | solution.py:40
  8.8 7.2 %collective-permute-start = (bf16[2,8,8,512]{3,2,1,0:T(8,128)(2,1)S(1)}, bf16[2,8,8,512]{3,2,1,0:T(8,128)(2,1)S(1)}, u32[]{:S(2)}, u32[]{:S(2)}) collective-permute-start(bf16[2,8,8,512]{3,2,1,0:T(8,128)(2,1)S(1)} %get-tuple-element.25), channel_id=1, source_target_pairs={{0,2},{2,0},{4,6},{6,4},{8,10},{10,8},{12,14},{14,12},{16,18},{18,... | collective-permute-start | bytes 393224 | tf_op jit(solution)/shard_map/ppermute | solution.py:40
  9.1 6.9 %collective-permute-start.1 = (bf16[2,8,8,512]{3,2,1,0:T(8,128)(2,1)S(1)}, bf16[2,8,8,512]{3,2,1,0:T(8,128)(2,1)S(1)}, u32[]{:S(2)}, u32[]{:S(2)}) collective-permute-start(bf16[2,8,8,512]{3,2,1,0:T(8,128)(2,1)S(1)} %get-tuple-element.26), channel_id=1, source_target_pairs={{2,4},{4,2},{6,8},{8,6},{10,12},{12,10},{14,16},{16,14},{18,20},{2... | collective-permute-start | bytes 393224 | tf_op jit(solution)/shard_map/ppermute | solution.py:40
  14.9 1.2 %collective-permute-start.3 = (bf16[2,8,8,512]{3,2,1,0:T(8,128)(2,1)S(1)}, bf16[2,8,8,512]{3,2,1,0:T(8,128)(2,1)S(1)}, u32[]{:S(2)}, u32[]{:S(2)}) collective-permute-start(bf16[2,8,8,512]{3,2,1,0:T(8,128)(2,1)S(1)} %get-tuple-element.32), channel_id=1, source_target_pairs={{4,8},{6,10},{8,4},{10,6},{12,16},{14,18},{16,12},{18,14},{20,24},... | collective-permute-start | bytes 393224 | tf_op jit(solution)/shard_map/ppermute | solution.py:40
  20.5 34.4 %copy-start = (bf16[640,1024]{1,0:T(8,128)(2,1)}, bf16[640,1024]{1,0:T(8,128)(2,1)S(1)}, u32[]{:S(2)}) copy-start(bf16[640,1024]{1,0:T(8,128)(2,1)S(1)} %get-tuple-element.34.px) | copy-start | bytes 3932164
  67.6 27.6 %all-to-all-start.2 = ((f32[32,32,128]{2,1,0:T(8,128)}), f32[32,32,128]{2,1,0:T(8,128)S(1)}, u32[]{:S(2)}, u32[]{:S(2)}) async-start(f32[32,32,128]{2,1,0:T(8,128)} %shard_map.92), calls=%async_computation.2 | async-start | bytes 1048576 | tf_op jit(solution)/shard_map/all_to_all | solution.py:501
  73.5 10.5 %collective-permute-start.4 = (bf16[2,8,8,512]{3,2,1,0:T(8,128)(2,1)S(1)}, bf16[2,8,8,512]{3,2,1,0:T(8,128)(2,1)S(1)}, u32[]{:S(2)}, u32[]{:S(2)}) collective-permute-start(bf16[2,8,8,512]{3,2,1,0:T(8,128)(2,1)S(1)} %get-tuple-element.37), channel_id=1, source_target_pairs={{0,2},{2,0},{4,6},{6,4},{8,10},{10,8},{12,14},{14,12},{16,18},{18,... | collective-permute-start | bytes 393224 | tf_op jit(solution)/shard_map/ppermute | solution.py:40
  74.9 18.7 %collective-permute-start.6 = (bf16[2,8,8,512]{3,2,1,0:T(8,128)(2,1)S(1)}, bf16[2,8,8,512]{3,2,1,0:T(8,128)(2,1)S(1)}, u32[]{:S(2)}, u32[]{:S(2)}) collective-permute-start(bf16[2,8,8,512]{3,2,1,0:T(8,128)(2,1)S(1)} %get-tuple-element.42), channel_id=1, source_target_pairs={{0,4},{2,6},{4,0},{6,2},{8,12},{10,14},{12,8},{14,10},{16,20},{18,... | collective-permute-start | bytes 393224 | tf_op jit(solution)/shard_map/ppermute | solution.py:40
  77.3 16.3 %collective-permute-start.5 = (bf16[2,8,8,512]{3,2,1,0:T(8,128)(2,1)S(1)}, bf16[2,8,8,512]{3,2,1,0:T(8,128)(2,1)S(1)}, u32[]{:S(2)}, u32[]{:S(2)}) collective-permute-start(bf16[2,8,8,512]{3,2,1,0:T(8,128)(2,1)S(1)} %get-tuple-element.40), channel_id=1, source_target_pairs={{2,4},{4,2},{6,8},{8,6},{10,12},{12,10},{14,16},{16,14},{18,20},{2... | collective-permute-start | bytes 393224 | tf_op jit(solution)/shard_map/ppermute | solution.py:40
  78.0 15.7 %collective-permute-start.7 = (bf16[2,8,8,512]{3,2,1,0:T(8,128)(2,1)S(1)}, bf16[2,8,8,512]{3,2,1,0:T(8,128)(2,1)S(1)}, u32[]{:S(2)}, u32[]{:S(2)}) collective-permute-start(bf16[2,8,8,512]{3,2,1,0:T(8,128)(2,1)S(1)} %get-tuple-element.44), channel_id=1, source_target_pairs={{4,8},{6,10},{8,4},{10,6},{12,16},{14,18},{16,12},{18,14},{20,24},... | collective-permute-start | bytes 393224 | tf_op jit(solution)/shard_map/ppermute | solution.py:40
  78.6 15.0 %copy-start.3 = (s32[1,4,2]{1,2,0:T(2,128)S(1)}, s32[1,4,2]{1,2,0:T(2,128)}, u32[]{:S(2)}) copy-start(s32[1,4,2]{1,2,0:T(2,128)} %param.11) | copy-start | bytes 100
where the time goes:
time: 96.7 us; the launch traced here: 96.2 us
  blocking collectives  46.1 us (48%)
  Pallas kernels  20 us (21%)
  starting transfers between devices  16.3 us (17%)
  waiting for transfers between devices  10.7 us (11%)
  other arithmetic  1.6 us (2%)
    all_to_all x1, blocking collectives, on_device(): lax.all_to_all(dwp.reshape(near, rows, 128), PLANE, 0, 0, tiled=True)  34.4 us
    all_to_all x1, blocking collectives, on_device(): parts = lax.all_to_all(total, 'z', 0, 0, tiled=True)  11.8 us
    ppermute x8, waiting for transfers between devices, swapped(): return lax.ppermute(block, SPACE, route)  10.7 us
    ppermute x8, starting transfers between devices, swapped(): return lax.ppermute(block, SPACE, route)  10.4 us
    all_to_all x1, starting transfers between devices, on_device(): packed = lax.all_to_all(total, PLANE, 0, 0, tiled=True).reshape(1024, 128)  5.86 us
    pallas_call x1, Pallas kernels, on_device(): call(dgrad_kernel, [VM, VM, SM, SM], (pltpu.VMEM((NB * 8, 8, 512), F32),...  5.08 us
    pallas_call x1, Pallas kernels, weight_pass(): call(wgrad_kernel, [VM] * 7 + [SM, SM], (shape((640, 1024), BF16), pltpu....  4.44 us
    pallas_call x1, Pallas kernels, on_device(): call(conv_kernel, [VM] * 3, BLOCK, [pltpu.VMEM((768, 384), BF16), pltpu.V...  4.29 us
  transfers between devices with their start and end apart: 9, of which 2 were waited for; matrix products, arithmetic and copies ran while one was open for 0% of the time, Pallas kernels for 12%

commit v1 on v0

--- a/solution.py
+++ b/solution.py
@@ -379,14 +379,14 @@
     total = parts[0]
     for n in range(1, parts.shape[0]):
         total = total + parts[n]
-    total = total * scale
+    total = (total * scale).astype(out.dtype)
     for n in range(out.shape[0]):
         out[n] = total
 
 
 def unpack_kernel(packed, out):
     for n in range(14):
-        tile = packed[64 * n : 64 * n + 64, :]
+        tile = packed[64 * n : 64 * n + 64, :].astype(F32)
         out[2 * n] = tile[:, 0:64]
         if 2 * n + 1 < 27:
             out[2 * n + 1] = pltpu.roll(tile, 64, 1)[:, 0:64]
@@ -420,9 +420,9 @@
     )
 
 
-def reduced(parts, copies, scale):
+def reduced(parts, copies, scale, dtype):
     rows = parts.shape[1]
-    out = pltpu.VMEM((copies, rows, 128), F32)
+    out = pltpu.VMEM((copies, rows, 128), dtype)
     kernel = functools.partial(sum_kernel, scale=scale)
     return call(kernel, [VM], out)(in_vmem(parts))
 
@@ -494,10 +494,10 @@
     rows = 1024 // near
     parts = lax.all_to_all(dwp.reshape(near, rows, 128), PLANE, 0, 0, tiled=True)
     returned[1] = swap(1, after(backs[1], dwp))
-    total = reduced(parts, far, 1.0)
+    total = reduced(parts, far, 1.0, F32)
     parts = lax.all_to_all(total, "z", 0, 0, tiled=True)
     returned[3] = swap(3, after(backs[3], total))
-    total = reduced(parts, near, scale)
+    total = reduced(parts, near, scale, BF16)
     packed = lax.all_to_all(total, PLANE, 0, 0, tiled=True).reshape(1024, 128)
     output = call(
         conv_kernel, [VM] * 3, BLOCK, [pltpu.VMEM((768, 384), BF16), pltpu.VMEM((4, 512, 384), F32)]

time: 96.7 us -> 93.6 us (0.968)
  the two profiles are of different devices: /device:TPU:1 before, /device:TPU:8 now
where the time goes in v1:
time: 93.6 us; the launch traced here: 93.1 us
  starting transfers between devices  30.5 us (33%)
  blocking collectives  28.9 us (31%)
  Pallas kernels  19.9 us (21%)
  waiting for transfers between devices  10.7 us (11%)
  other arithmetic  1.6 us (2%)
    ppermute x8, starting transfers between devices, swapped(): return lax.ppermute(block, SPACE, route)  25.4 us
    all_to_all x1, blocking collectives, on_device(): lax.all_to_all(dwp.reshape(near, rows, 128), PLANE, 0, 0, tiled=True)  14.6 us
    all_to_all x1, blocking collectives, on_device(): parts = lax.all_to_all(total, 'z', 0, 0, tiled=True)  14.3 us
    ppermute x8, waiting for transfers between devices, swapped(): return lax.ppermute(block, SPACE, route)  10.7 us
    all_to_all x1, starting transfers between devices, on_device(): packed = lax.all_to_all(total, PLANE, 0, 0, tiled=True).reshape(1024, 128)  5.12 us
    pallas_call x1, Pallas kernels, on_device(): call(dgrad_kernel, [VM, VM, SM, SM], (pltpu.VMEM((NB * 8, 8, 512), F32),...  5.09 us
    pallas_call x1, Pallas kernels, weight_pass(): call(wgrad_kernel, [VM] * 7 + [SM, SM], (shape((640, 1024), BF16), pltpu....  4.43 us
    pallas_call x1, Pallas kernels, on_device(): call(conv_kernel, [VM] * 3, BLOCK, [pltpu.VMEM((768, 384), BF16), pltpu.V...  4.28 us
  transfers between devices with their start and end apart: 9, of which 3 were waited for; matrix products, arithmetic and copies ran while one was open for 0% of the time, Pallas kernels for 12%

profile of v1, /device:TPU:8, one launch (start us, length us, event | category | flops | bytes accessed | tf_op | source)
XLA Modules:
  0.0 93.1 jit_solution(4651989568986538050)
XLA Ops:
  0.6 0.0 copy-start.1
  0.6 1.6 %fusion.2 = bf16[9,4,64,128]{3,2,1,0:T(8,128)(2,1)S(1)} fusion(bf16[9,3,64,64]{3,2,1,0:T(8,128)(2,1)} %bitcast.14), kind=kLoop, calls=%fused_computation.4 | loop fusion | flops 2359296 | bytes 811008 | tf_op jit(solution)/shard_map/concatenate | solution.py:468
  2.2 0.0 copy-start.2
  2.3 0.7 copy-done.2
  2.9 2.2 %shard_map.85 = (bf16[6,8,8,512]{3,2,1,0:T(8,128)(2,1)S(1)}, bf16[6,8,8,512]{3,2,1,0:T(8,128)(2,1)S(1)}, bf16[8,48,512]{2,1,0:T(8,128)(2,1)S(1)}, bf16[2,8,8,512...) custom-call(bf16[6,8,8,512]{3,2,1,0:T(8,128)(2,1)} %feat_far.1, ...), custom_call_target="tpu_custom_call" | custom-call | tf_op jit(solution)/shard_map/pallas_call | solution.py:448
  5.2 3.1 %collective-permute-start.2 = (bf16[2,8,8,512]{3,2,1,0:T(8,128)(2,1)S(1)}, bf16[2,8,8,512]{3,2,1,0:T(8,128)(2,1)S(1)}, u32[]{:S(2)}, u32[]{:S(2)}) collective-permute-start(bf16[2,8,8,512]{3,2,1,0:T(8,128)(2,1)S(1)} %get-tuple-element.28), channel_id=1, source_target_pairs={{0,4},{2,6},{4,0},{6,2},{8,12},{10,14},{12,8},{14,10},{16,20},{18,... | collective-permute-start | bytes 393224 | tf_op jit(solution)/shard_map/ppermute | solution.py:40
  8.3 0.6 collective-permute-start
  8.9 7.6 %collective-permute-start.1 = (bf16[2,8,8,512]{3,2,1,0:T(8,128)(2,1)S(1)}, bf16[2,8,8,512]{3,2,1,0:T(8,128)(2,1)S(1)}, u32[]{:S(2)}, u32[]{:S(2)}) collective-permute-start(bf16[2,8,8,512]{3,2,1,0:T(8,128)(2,1)S(1)} %get-tuple-element.26), channel_id=1, source_target_pairs={{2,4},{4,2},{6,8},{8,6},{10,12},{12,10},{14,16},{16,14},{18,20},{2... | collective-permute-start | bytes 393224 | tf_op jit(solution)/shard_map/ppermute | solution.py:40
  16.5 0.0 copy-done.1
  16.5 5.1 %shard_map.86 = (f32[48,8,512]{2,1,0:T(8,128)S(1)}, bf16[2,8,8,512]{3,2,1,0:T(8,128)(2,1)S(1)}, bf16[2,8,8,512]{3,2,1,0:T(8,128)(2,1)S(1)}, bf16[2,8,8,512]{3,2,1,0:T(8,128)(2,1)S(1)}, bf16[2,8,8,512]{3,2,1,0:T(8,128)(2,1)S(1)}) custom-call(bf16[8,48,512]{2,1,0:T(8,128)(2,1)S(1)} %get-tuple-element.33.g, bf16[36,64,128]{2,1,0:T(8,128)(2,1)S(1)} %bitcast.7, ...), custom_call_target="tpu_custom_call" | custom-call | tf_op jit(solution)/shard_map/pallas_call | solution.py:472
  21.6 4.9 %collective-permute-start.3 = (bf16[2,8,8,512]{3,2,1,0:T(8,128)(2,1)S(1)}, bf16[2,8,8,512]{3,2,1,0:T(8,128)(2,1)S(1)}, u32[]{:S(2)}, u32[]{:S(2)}) collective-permute-start(bf16[2,8,8,512]{3,2,1,0:T(8,128)(2,1)S(1)} %get-tuple-element.32), channel_id=1, source_target_pairs={{4,8},{6,10},{8,4},{10,6},{12,16},{14,18},{16,12},{18,14},{20,24},... | collective-permute-start | bytes 393224 | tf_op jit(solution)/shard_map/ppermute | solution.py:40
  26.5 0.5 shard_map.87.gext
  27.0 0.0 collective-permute-done.2.a2
  27.0 0.0 collective-permute-done.a0
  27.0 0.0 collective-permute-done.1.a1
  27.0 6.0 %collective-permute-done.3.a3 = bf16[2,8,8,512]{3,2,1,0:T(8,128)(2,1)S(1)} collective-permute-done((bf16[2,8,8,512]{3,2,1,0:T(8,128)(2,1)S(1)}, bf16[2,8,8,512]{3,2,1,0:T(8,128)(2,1)S(1)}, u32[]{:S(2)}, u32[]{:S(2)}) %collective-permute-start.3) | collective-permute-done | bytes 131104 | tf_op jit(solution)/shard_map/ppermute | solution.py:40
  33.0 4.4 %shard_map.88 = (bf16[640,1024]{1,0:T(8,128)(2,1)S(1)}, f32[1024,128]{1,0:T(8,128)S(1)}) custom-call(bf16[6,8,8,512]{3,2,1,0:T(8,128)(2,1)S(1)} %get-tuple-element.24.shown, bf16[2,8,8,512]{3,2,1,0:T(8,128)(2,1)S(1)} %collective-permute-done.a0, bf16[2,8,8,512]{3,2,1,0:T(8,128)(2,1)S(1)} %collective-permute-done.1.a1, ...), custom_call_target="tpu_custom_call" | custom-call | tf_op jit(solution)/shard_map/pallas_call | solution.py:432
  37.4 0.0 copy-start
  37.4 14.6 %all_to_all.15.parts = f32[32,32,128]{2,1,0:T(8,128)S(1)} all-to-all(f32[32,32,128]{2,1,0:T(8,128)S(1)} %bitcast.10), channel_id=1, replica_groups=mesh['y'=4,'z'=8,'x'=4,'dp'=2] {'y','x','dp'}, dimensions={0} | all-to-all | bytes 1048576 | tf_op jit(solution)/shard_map/all_to_all | solution.py:495
  52.1 0.0 copy-done
  52.1 14.3 %all_to_all.16.parts = f32[8,32,128]{2,1,0:T(8,128)S(1)} all-to-all(f32[8,32,128]{2,1,0:T(8,128)S(1)} %shard_map.90), channel_id=1, replica_groups=mesh['y'=4,'z'=8,'x'=4,'dp'=2] {'z'}, dimensions={0} | all-to-all | bytes 262144 | tf_op jit(solution)/shard_map/all_to_all | solution.py:498
  66.4 0.7 shard_map.92
  67.2 5.1 %all-to-all-start.2 = ((bf16[32,32,128]{2,1,0:T(8,128)(2,1)}), bf16[32,32,128]{2,1,0:T(8,128)(2,1)S(1)}, u32[]{:S(2)}, u32[]{:S(2)}) async-start(bf16[32,32,128]{2,1,0:T(8,128)(2,1)} %shard_map.92), calls=%async_computation.2 | async-start | bytes 524288 | tf_op jit(solution)/shard_map/all_to_all | solution.py:501
  72.3 1.6 %collective-permute-start.4 = (bf16[2,8,8,512]{3,2,1,0:T(8,128)(2,1)S(1)}, bf16[2,8,8,512]{3,2,1,0:T(8,128)(2,1)S(1)}, u32[]{:S(2)}, u32[]{:S(2)}) collective-permute-start(bf16[2,8,8,512]{3,2,1,0:T(8,128)(2,1)S(1)} %get-tuple-element.37), channel_id=1, source_target_pairs={{0,2},{2,0},{4,6},{6,4},{8,10},{10,8},{12,14},{14,12},{16,18},{18,... | collective-permute-start | bytes 393224 | tf_op jit(solution)/shard_map/ppermute | solution.py:40
  73.8 2.7 %collective-permute-start.6 = (bf16[2,8,8,512]{3,2,1,0:T(8,128)(2,1)S(1)}, bf16[2,8,8,512]{3,2,1,0:T(8,128)(2,1)S(1)}, u32[]{:S(2)}, u32[]{:S(2)}) collective-permute-start(bf16[2,8,8,512]{3,2,1,0:T(8,128)(2,1)S(1)} %get-tuple-element.42), channel_id=1, source_target_pairs={{0,4},{2,6},{4,0},{6,2},{8,12},{10,14},{12,8},{14,10},{16,20},{18,... | collective-permute-start | bytes 393224 | tf_op jit(solution)/shard_map/ppermute | solution.py:40
  76.5 1.9 %collective-permute-start.5 = (bf16[2,8,8,512]{3,2,1,0:T(8,128)(2,1)S(1)}, bf16[2,8,8,512]{3,2,1,0:T(8,128)(2,1)S(1)}, u32[]{:S(2)}, u32[]{:S(2)}) collective-permute-start(bf16[2,8,8,512]{3,2,1,0:T(8,128)(2,1)S(1)} %get-tuple-element.40), channel_id=1, source_target_pairs={{2,4},{4,2},{6,8},{8,6},{10,12},{12,10},{14,16},{16,14},{18,20},{2... | collective-permute-start | bytes 393224 | tf_op jit(solution)/shard_map/ppermute | solution.py:40
  78.4 3.1 %collective-permute-start.7 = (bf16[2,8,8,512]{3,2,1,0:T(8,128)(2,1)S(1)}, bf16[2,8,8,512]{3,2,1,0:T(8,128)(2,1)S(1)}, u32[]{:S(2)}, u32[]{:S(2)}) collective-permute-start(bf16[2,8,8,512]{3,2,1,0:T(8,128)(2,1)S(1)} %get-tuple-element.44), channel_id=1, source_target_pairs={{4,8},{6,10},{8,4},{10,6},{12,16},{14,18},{16,12},{18,14},{20,24},... | collective-permute-start | bytes 393224 | tf_op jit(solution)/shard_map/ppermute | solution.py:40
  81.5 0.0 copy-start.3
  81.5 4.3 %shard_map.89 = bf16[6,8,8,512]{3,2,1,0:T(8,128)(2,1)} custom-call(bf16[640,1024]{1,0:T(8,128)(2,1)} %copy-done, bf16[36,64,128]{2,1,0:T(8,128)(2,1)S(1)} %bitcast.8, bf16[6,8,8,512]{3,2,1,0:T(8,128)(2,1)S(1)} %get-tuple-element.35.live), custom_call_target="tpu_custom_call" | custom-call | tf_op jit(solution)/shard_map/pallas_call | solution.py:502
  85.8 0.0 collective-permute-done.4.a0
  85.8 0.0 collective-permute-done.6.a2
  85.8 3.3 %collective-permute-done.5.a1 = bf16[2,8,8,512]{3,2,1,0:T(8,128)(2,1)S(1)} collective-permute-done((bf16[2,8,8,512]{3,2,1,0:T(8,128)(2,1)S(1)}, bf16[2,8,8,512]{3,2,1,0:T(8,128)(2,1)S(1)}, u32[]{:S(2)}, u32[]{:S(2)}) %collective-permute-start.5) | collective-permute-done | bytes 131104 | tf_op jit(solution)/shard_map/ppermute | solution.py:40
  89.1 1.4 %collective-permute-done.7.a3 = bf16[2,8,8,512]{3,2,1,0:T(8,128)(2,1)S(1)} collective-permute-done((bf16[2,8,8,512]{3,2,1,0:T(8,128)(2,1)S(1)}, bf16[2,8,8,512]{3,2,1,0:T(8,128)(2,1)S(1)}, u32[]{:S(2)}, u32[]{:S(2)}) %collective-permute-start.7) | collective-permute-done | bytes 131104 | tf_op jit(solution)/shard_map/ppermute | solution.py:40
  90.5 0.0 copy-done.3
  90.5 1.5 %shard_map.91 = bf16[6,8,8,512]{3,2,1,0:T(8,128)(2,1)} custom-call(f32[48,8,512]{2,1,0:T(8,128)S(1)} %get-tuple-element.31.before.rloc, bf16[2,8,8,512]{3,2,1,0:T(8,128)(2,1)S(1)} %collective-permute-done.4.a0, bf16[2,8,8,512]{3,2,1,0:T(8,128)(2,1)S(1)} %collective-permute-done.5.a1, bf16[2,8,8,512]{3,2,1,0:T(8,128)(2,1)S(1)} %collective-permute-done.6.a2, ...), custom_call_target="tpu_custom_call" | custom-call | tf_op jit(solution)/shard_map/pallas_call | solution.py:506
  92.1 0.0 all-to-all-done.2
  92.1 1.0 %shard_map.93 = f32[27,64,64]{2,1,0:T(8,128)} custom-call(bf16[1024,128]{1,0:T(8,128)(2,1)S(1)} %bitcast.9), custom_call_target="tpu_custom_call" | custom-call | tf_op jit(solution)/shard_map/pallas_call | solution.py:505
  (1 shorter events, 0.0 us)
Async XLA Ops:
  0.6 15.9 %copy-start.1 = (s32[6,26]{1,0:T(8,128)S(1)}, s32[6,26]{1,0:T(8,128)}, u32[]{:S(2)}) copy-start(s32[6,26]{1,0:T(8,128)} %nbr.3) | copy-start | bytes 1876
  2.2 0.7 copy-start.2
  5.2 21.8 %collective-permute-start.2 = (bf16[2,8,8,512]{3,2,1,0:T(8,128)(2,1)S(1)}, bf16[2,8,8,512]{3,2,1,0:T(8,128)(2,1)S(1)}, u32[]{:S(2)}, u32[]{:S(2)}) collective-permute-start(bf16[2,8,8,512]{3,2,1,0:T(8,128)(2,1)S(1)} %get-tuple-element.28), channel_id=1, source_target_pairs={{0,4},{2,6},{4,0},{6,2},{8,12},{10,14},{12,8},{14,10},{16,20},{18,... | collective-permute-start | bytes 393224 | tf_op jit(solution)/shard_map/ppermute | solution.py:40
  8.3 18.7 %collective-permute-start = (bf16[2,8,8,512]{3,2,1,0:T(8,128)(2,1)S(1)}, bf16[2,8,8,512]{3,2,1,0:T(8,128)(2,1)S(1)}, u32[]{:S(2)}, u32[]{:S(2)}) collective-permute-start(bf16[2,8,8,512]{3,2,1,0:T(8,128)(2,1)S(1)} %get-tuple-element.25), channel_id=1, source_target_pairs={{0,2},{2,0},{4,6},{6,4},{8,10},{10,8},{12,14},{14,12},{16,18},{18,... | collective-permute-start | bytes 393224 | tf_op jit(solution)/shard_map/ppermute | solution.py:40
  8.9 18.1 %collective-permute-start.1 = (bf16[2,8,8,512]{3,2,1,0:T(8,128)(2,1)S(1)}, bf16[2,8,8,512]{3,2,1,0:T(8,128)(2,1)S(1)}, u32[]{:S(2)}, u32[]{:S(2)}) collective-permute-start(bf16[2,8,8,512]{3,2,1,0:T(8,128)(2,1)S(1)} %get-tuple-element.26), channel_id=1, source_target_pairs={{2,4},{4,2},{6,8},{8,6},{10,12},{12,10},{14,16},{16,14},{18,20},{2... | collective-permute-start | bytes 393224 | tf_op jit(solution)/shard_map/ppermute | solution.py:40
  21.6 11.4 %collective-permute-start.3 = (bf16[2,8,8,512]{3,2,1,0:T(8,128)(2,1)S(1)}, bf16[2,8,8,512]{3,2,1,0:T(8,128)(2,1)S(1)}, u32[]{:S(2)}, u32[]{:S(2)}) collective-permute-start(bf16[2,8,8,512]{3,2,1,0:T(8,128)(2,1)S(1)} %get-tuple-element.32), channel_id=1, source_target_pairs={{4,8},{6,10},{8,4},{10,6},{12,16},{14,18},{16,12},{18,14},{20,24},... | collective-permute-start | bytes 393224 | tf_op jit(solution)/shard_map/ppermute | solution.py:40
  37.4 14.7 %copy-start = (bf16[640,1024]{1,0:T(8,128)(2,1)}, bf16[640,1024]{1,0:T(8,128)(2,1)S(1)}, u32[]{:S(2)}) copy-start(bf16[640,1024]{1,0:T(8,128)(2,1)S(1)} %get-tuple-element.34.px) | copy-start | bytes 3932164
  67.2 24.9 %all-to-all-start.2 = ((bf16[32,32,128]{2,1,0:T(8,128)(2,1)}), bf16[32,32,128]{2,1,0:T(8,128)(2,1)S(1)}, u32[]{:S(2)}, u32[]{:S(2)}) async-start(bf16[32,32,128]{2,1,0:T(8,128)(2,1)} %shard_map.92), calls=%async_computation.2 | async-start | bytes 524288 | tf_op jit(solution)/shard_map/all_to_all | solution.py:501
  72.3 13.5 %collective-permute-start.4 = (bf16[2,8,8,512]{3,2,1,0:T(8,128)(2,1)S(1)}, bf16[2,8,8,512]{3,2,1,0:T(8,128)(2,1)S(1)}, u32[]{:S(2)}, u32[]{:S(2)}) collective-permute-start(bf16[2,8,8,512]{3,2,1,0:T(8,128)(2,1)S(1)} %get-tuple-element.37), channel_id=1, source_target_pairs={{0,2},{2,0},{4,6},{6,4},{8,10},{10,8},{12,14},{14,12},{16,18},{18,... | collective-permute-start | bytes 393224 | tf_op jit(solution)/shard_map/ppermute | solution.py:40
  73.8 12.0 %collective-permute-start.6 = (bf16[2,8,8,512]{3,2,1,0:T(8,128)(2,1)S(1)}, bf16[2,8,8,512]{3,2,1,0:T(8,128)(2,1)S(1)}, u32[]{:S(2)}, u32[]{:S(2)}) collective-permute-start(bf16[2,8,8,512]{3,2,1,0:T(8,128)(2,1)S(1)} %get-tuple-element.42), channel_id=1, source_target_pairs={{0,4},{2,6},{4,0},{6,2},{8,12},{10,14},{12,8},{14,10},{16,20},{18,... | collective-permute-start | bytes 393224 | tf_op jit(solution)/shard_map/ppermute | solution.py:40
  76.5 12.6 %collective-permute-start.5 = (bf16[2,8,8,512]{3,2,1,0:T(8,128)(2,1)S(1)}, bf16[2,8,8,512]{3,2,1,0:T(8,128)(2,1)S(1)}, u32[]{:S(2)}, u32[]{:S(2)}) collective-permute-start(bf16[2,8,8,512]{3,2,1,0:T(8,128)(2,1)S(1)} %get-tuple-element.40), channel_id=1, source_target_pairs={{2,4},{4,2},{6,8},{8,6},{10,12},{12,10},{14,16},{16,14},{18,20},{2... | collective-permute-start | bytes 393224 | tf_op jit(solution)/shard_map/ppermute | solution.py:40
  78.4 12.1 %collective-permute-start.7 = (bf16[2,8,8,512]{3,2,1,0:T(8,128)(2,1)S(1)}, bf16[2,8,8,512]{3,2,1,0:T(8,128)(2,1)S(1)}, u32[]{:S(2)}, u32[]{:S(2)}) collective-permute-start(bf16[2,8,8,512]{3,2,1,0:T(8,128)(2,1)S(1)} %get-tuple-element.44), channel_id=1, source_target_pairs={{4,8},{6,10},{8,4},{10,6},{12,16},{14,18},{16,12},{18,14},{20,24},... | collective-permute-start | bytes 393224 | tf_op jit(solution)/shard_map/ppermute | solution.py:40
  81.5 9.0 %copy-start.3 = (s32[1,4,2]{1,2,0:T(2,128)S(1)}, s32[1,4,2]{1,2,0:T(2,128)}, u32[]{:S(2)}) copy-start(s32[1,4,2]{1,2,0:T(2,128)} %param.11) | copy-start | bytes 100
